TPU v7x, 256 devices: a whole 4x4x8 slice. The times are simulated.
256 devices in a mesh: pair: 2 (over core), virt: 4 (over x), integ: 32 (over y, z).
Axes of the slice: x: 4, y: 4, z: 8, core: 2. Of those that a mesh axis runs over, the one named last changes fastest.
Arguments:
- amplitudes: bfloat16 [2, 32, 256, 256], P('pair', 'integ', 'virt'), may hold values from -4 to 4
- vv_factors: bfloat16 [512, 256, 256], P('integ'), may hold values from -0.25 to 0.25
- ov_factors: bfloat16 [512, 32, 256], P(None, 'integ'), may hold values from -0.75 to 0.75
- occ_energy_i: float32 [2], P('pair'), may hold values from -2 to -0.5
- occ_energy_j: float32 [32], P('integ'), may hold values from -2 to -0.5
- virt_energy: float32 [256], replicated, may hold values from 0.2 to 3
- vv_mask: int32 [2, 2], replicated, may hold values 0 or 1
- pair_domain: int32 [2, 32, 2], P('pair', 'integ'), may hold values 0 or 1
Outputs:
- update: bfloat16 [2, 32, 256, 256], P('pair', 'integ', 'virt')
All inputs are finite; a program needn't handle non-finite values. No bound on the sum of `pair_domain` on one device may be relied on, other than what follows from the above.
Results may differ from a plain program's by a relative error of at most 0.014.
Values may be sent and summed in bfloat16 or wider, within the bound.
No kernel may reach another device: no remote copies, remote signals or barrier semaphores. Data moves between devices by JAX's collectives and lax.ppermute only.
A program may use at most 64 MiB of HBM per device.

v0:
```python
import jax
import jax.numpy as jnp
from jax import lax
from jax.sharding import PartitionSpec as P

TILE_SIZE = 128


def split_halves(values):
    upper = values.astype(jnp.bfloat16)
    lower = (values - upper.astype(jnp.float32)).astype(jnp.bfloat16)
    return (upper, lower)


def body(
    amplitudes,
    vv_factors,
    ov_factors,
    occ_energy_i,
    occ_energy_j,
    virt_energy,
    vv_mask,
    pair_domain,
):
    share = amplitudes.shape[2]
    virt_index = lax.axis_index("virt")
    row_start = virt_index * share
    domain = jnp.repeat(pair_domain[0, 0], TILE_SIZE).astype(jnp.float32)
    domain_rows = lax.dynamic_slice_in_dim(domain, row_start, share, 0)
    masked = (amplitudes[0, 0].astype(jnp.float32) * domain_rows[:, None] * domain[None, :]).astype(
        jnp.bfloat16
    )
    grid = jnp.repeat(jnp.repeat(vv_mask, TILE_SIZE, axis=0), TILE_SIZE, axis=1).astype(
        jnp.bfloat16
    )
    factors = vv_factors * grid[None]
    factor_rows = lax.dynamic_slice_in_dim(factors, row_start, share, 1)
    masked_block = masked[None, None]
    full_rows = lax.all_gather(masked_block, "virt", axis=2, tiled=True)
    own_pair = full_rows[0, 0]
    all_pairs = lax.all_gather(full_rows, "integ", axis=1, tiled=True)[0]
    columns = lax.dynamic_slice_in_dim(own_pair, row_start, share, 1)
    mixed = (2.0 * masked.astype(jnp.float32) - columns.T.astype(jnp.float32)).astype(jnp.bfloat16)
    own_ov = ov_factors[:, 0, :]
    partial_zeta = jnp.einsum("ac,qc->aq", mixed, own_ov, preferred_element_type=jnp.float32)
    pieces = []
    for first in range(0, lax.axis_size("integ") * 1, 8):
        width = min(8, lax.axis_size("integ") * 1 - first)
        block = lax.dynamic_slice_in_dim(all_pairs, first, width, 0)
        weighted = jnp.einsum(
            "qac,jcd->jqad", factor_rows, block, preferred_element_type=jnp.float32
        ).astype(jnp.bfloat16)
        pieces.append(
            jnp.einsum("jqad,qbd->jab", weighted, factors, preferred_element_type=jnp.float32)
        )
    term = jnp.concatenate(pieces, axis=0)
    ladder = lax.psum_scatter(
        term.astype(jnp.bfloat16), "integ", scatter_dimension=0, tiled=True
    ).astype(jnp.float32)[0]
    zeta = lax.psum(partial_zeta, "integ")
    upper, lower = split_halves(zeta)
    cycle = jnp.dot(upper, own_ov, preferred_element_type=jnp.float32)
    cycle = cycle + jnp.dot(lower, own_ov, preferred_element_type=jnp.float32)
    total = ladder + cycle
    energy_rows = lax.dynamic_slice_in_dim(virt_energy, row_start, share, 0)
    denom = energy_rows[:, None] + virt_energy[None, :] - occ_energy_i[0] - occ_energy_j[0]
    update = (total * domain_rows[:, None] * domain[None, :] / denom).astype(jnp.bfloat16)
    return update[None, None]


def solution(mesh):
    placed = (
        P("pair", "integ", "virt", None),
        P("integ", None, None),
        P(None, "integ", None),
        P("pair"),
        P("integ"),
        P(),
        P(),
        P("pair", "integ", None),
    )
    return jax.shard_map(
        body,
        mesh=mesh,
        in_specs=placed,
        out_specs=P("pair", "integ", "virt", None),
        check_vma=False,
    )
```

profile of v0, /device:TPU:2, one launch (start us, length us, event | category | flops | bytes accessed | tf_op | source)
XLA Modules:
  0.0 472.5 jit_solution(15324939264644739411)
XLA Ops:
  6.5 0.0 copy-start
  6.5 0.0 all-gather.2.cloned.1.call-start
  6.5 0.7 convert_bitcast_fusion.2
  7.2 0.1 broadcast_bitcast_fusion
  7.3 0.1 dynamic_slice.32
  7.4 0.8 fusion.92
  8.2 12.8 %all_gather.6 = bf16[1,1,256,256]{3,2,1,0:T(8,128)(2,1)} all-gather(bf16[1,1,64,256]{3,2,1,0:T(8,128)(2,1)S(1)} %fusion.92), channel_id=1, replica_groups=mesh['pair'=2,'virt'=4,'integ'=32] {'virt'}, dimensions={2}, use_global_device_ids=true | all-gather | bytes 163840 | tf_op jit(solution)/shard_map/all_gather | solution.py:39
  21.0 0.0 all-gather.2.cloned.1.call-update
  21.1 0.0 all-reduce.2.cloned.1.call-start
  21.1 0.9 constant_dynamic-slice_fusion
  22.1 0.1 copy.22
  22.2 0.0 copy-done
  22.2 1.6 fusion.89
  23.8 0.0 all-reduce.2.cloned.1.call-update
  23.8 0.0 reduce-scatter.2.cloned.1.call-start
  23.9 0.7 convert_element_type.102
  24.6 0.3 broadcast_in_dim.10
  24.9 1.8 broadcast_multiply_fusion
  26.7 78.9 %all-gather.2.cloned.1.call-done = bf16[1,32,256,256]{3,2,0,1:T(8,128)(2,1)} async-done(((bf16[1,1,256,256]{3,2,0,1:T(8,128)(2,1)}), bf16[1,32,256,256]{3,2,0,1:T(8,128)(2,1)}) %all-gather.2.cloned.1.call-update) | async-done | bytes 4194320 | tf_op jit(solution)/shard_map/all_gather | solution.py:41
  105.6 5.4 %fusion.44 = bf16[8,64,256]{2,1,0:T(8,128)(2,1)S(1)} fusion(bf16[16,256,256]{2,1,0:T(8,128)(2,1)S(1)} %broadcast_multiply_fusion, bf16[1,32,256,256]{3,2,0,1:T(8,128)(2,1)} %all-gather.2.cloned.1.call-done, s32[]{:T(128)S(6)} %select_n.2), kind=kOutput, calls=%fused_computation.24 | convolution fusion | flops 2149711872 | bytes 3932164 | tf_op jit(solution)/shard_map/jqad,qbd->jab/dot_general | solution.py:54
  111.1 5.4 %fusion.49 = bf16[8,64,256]{2,1,0:T(8,128)(2,1)S(1)} fusion(bf16[16,256,256]{2,1,0:T(8,128)(2,1)S(1)} %broadcast_multiply_fusion, bf16[1,32,256,256]{3,2,0,1:T(8,128)(2,1)} %all-gather.2.cloned.1.call-done, s32[]{:T(128)S(6)} %select_n.2), kind=kOutput, calls=%fused_computation.25 | convolution fusion | flops 2149711872 | bytes 3932164 | tf_op jit(solution)/shard_map/jqad,qbd->jab/dot_general | solution.py:54
  116.5 5.5 %fusion.54 = bf16[8,64,256]{2,1,0:T(8,128)(2,1)S(1)} fusion(bf16[16,256,256]{2,1,0:T(8,128)(2,1)S(1)} %broadcast_multiply_fusion, bf16[1,32,256,256]{3,2,0,1:T(8,128)(2,1)} %all-gather.2.cloned.1.call-done, s32[]{:T(128)S(6)} %select_n.2), kind=kOutput, calls=%fused_computation.26 | convolution fusion | flops 2149711872 | bytes 3932164 | tf_op jit(solution)/shard_map/jqad,qbd->jab/dot_general | solution.py:54
  122.0 0.0 copy-start.1
  122.0 5.5 %fusion.59 = bf16[8,64,256]{2,1,0:T(8,128)(2,1)S(1)} fusion(bf16[16,256,256]{2,1,0:T(8,128)(2,1)S(1)} %broadcast_multiply_fusion, bf16[1,32,256,256]{3,2,0,1:T(8,128)(2,1)} %all-gather.2.cloned.1.call-done, s32[]{:T(128)S(6)} %select_n.2), kind=kOutput, calls=%fused_computation.27 | convolution fusion | flops 2149711872 | bytes 3932164 | tf_op jit(solution)/shard_map/jqad,qbd->jab/dot_general | solution.py:54
  127.5 1.1 pad_maximum_fusion
  128.6 0.0 reduce-scatter.2.cloned.1.call-update
  128.6 0.0 copy-done.1
  128.6 0.1 dynamic_slice.43
  130.0 117.1 %all-reduce.2.cloned.1.call-done = f32[64,512]{1,0:T(8,128)} async-done(((f32[64,512]{1,0:T(8,128)}), f32[64,512]{1,0:T(8,128)}) %all-reduce.2.cloned.1.call-update) | async-done | bytes 131088 | tf_op jit(solution)/shard_map/psum | solution.py:60
  247.1 1.1 fusion.87
  248.2 216.0 %reduce-scatter.2.cloned.1.call-done = bf16[1,64,256]{2,1,0:T(8,128)(2,1)} async-done(((bf16[32,64,256]{2,1,0:T(8,128)(2,1)}), bf16[1,64,256]{2,1,0:T(8,128)(2,1)}) %reduce-scatter.2.cloned.1.call-update) | async-done | bytes 32784 | tf_op jit(solution)/shard_map/reduce_scatter | solution.py:57
  464.2 1.8 fusion.69
  (2 shorter events, 0.0 us)
Async XLA Ops:
  6.5 15.6 %copy-start = (bf16[512,1,256]{2,0,1:T(8,128)(2,1)S(1)}, bf16[512,1,256]{2,0,1:T(8,128)(2,1)}, u32[]{:S(2)}) copy-start(bf16[512,1,256]{2,0,1:T(8,128)(2,1)} %param.10) | copy-start | bytes 786436
  6.5 99.1 %all-gather.2.cloned.1.call-start = ((), (), s32[]{:S(2)}) async-start(), calls=%async_computation.1 | async-start | bytes 4325376 | tf_op jit(solution)/shard_map/all_gather | solution.py:41
  21.1 226.1 %all-reduce.2.cloned.1.call-start = ((), (), s32[]{:S(2)}) async-start(), calls=%async_computation.3 | async-start | bytes 262144 | tf_op jit(solution)/shard_map/psum | solution.py:60
  23.8 440.4 %reduce-scatter.2.cloned.1.call-start = ((), (), s32[]{:S(2)}) async-start(), calls=%async_computation.2 | async-start | bytes 1081344 | tf_op jit(solution)/shard_map/reduce_scatter | solution.py:57
  122.0 6.6 %copy-start.1 = (f32[256]{0:T(256)S(1)}, f32[256]{0:T(256)}, u32[]{:S(2)}) copy-start(f32[256]{0:T(256)} %param.13) | copy-start | bytes 3076
Sparse Core Ops, SparseCore 0:
  21.2 84.4 all-gather.1
  109.1 137.9 all-reduce.1
  251.4 212.6 reduce-scatter.1
where the time goes:
time: 473 us; the launch traced here: 472 us
  waiting for transfers between devices  412 us (87%)
  matrix products  26.3 us (6%)
  between operations  14.5 us (3%)
  blocking collectives  12.8 us (3%)
  other arithmetic  5.11 us (1%)
    reduce_scatter x1, waiting for transfers between devices, body(): lax.psum_scatter(term.astype(jnp.bfloat16), 'integ', scatter_dimension=0,...  216 us
    psum x1, waiting for transfers between devices, body(): zeta = lax.psum(partial_zeta, 'integ')  117 us
    all_gather x1, waiting for transfers between devices, body(): all_pairs = lax.all_gather(full_rows, 'integ', axis=1, tiled=True)[0]  78.9 us
    dot_general x4, matrix products, body(): jnp.einsum('jqad,qbd->jab', weighted, factors, preferred_element_type=jnp...  21.8 us
    all_gather x1, blocking collectives, body(): full_rows = lax.all_gather(masked_block, 'virt', axis=2, tiled=True)  12.8 us
  transfers between devices with their start and end apart: 3, of which 3 were waited for; matrix products, arithmetic and copies ran while one was open for 6% of the time, Pallas kernels for 0%

commit v1 on v0

--- a/solution.py
+++ b/solution.py
@@ -57,7 +57,12 @@
     ladder = lax.psum_scatter(
         term.astype(jnp.bfloat16), "integ", scatter_dimension=0, tiled=True
     ).astype(jnp.float32)[0]
-    zeta = lax.psum(partial_zeta, "integ")
+
+    def watch_tails(state, mesh_ax):
+        local_now = lax.all_gather(state, axis_name=mesh_ax)
+        return jnp.sum(local_now, axis=0)
+
+    zeta = watch_tails(partial_zeta, "integ")
     upper, lower = split_halves(zeta)
     cycle = jnp.dot(upper, own_ov, preferred_element_type=jnp.float32)
     cycle = cycle + jnp.dot(lower, own_ov, preferred_element_type=jnp.float32)

time: 473 us -> 411 us (0.87)
  waiting for transfers between devices: 412 us -> 349 us
    psum x1 -> x0, waiting for transfers between devices: 117 us -> none  [body(): zeta = lax.psum(partial_zeta, 'integ')]
    all_gather x0 -> x1, waiting for transfers between devices: none -> 57.3 us  [watch_tails(): local_now = lax.all_gather(state, axis_name=mesh_ax)]
  transfers between devices with their start and end apart: 3 -> 3, of which waited for: 3 -> 3; matrix products, arithmetic and copies ran while one was open for 6% -> 8% of each run, Pallas kernels for 0% -> 0%
where the time goes in v1:
time: 411 us
  waiting for transfers between devices  349 us (85%)
  matrix products  25.1 us (6%)
  between operations  14.5 us (4%)
  blocking collectives  12.8 us (3%)
  other arithmetic  7.65 us (2%)
    reduce_scatter x1, waiting for transfers between devices, body(): lax.psum_scatter(term.astype(jnp.bfloat16), 'integ', scatter_dimension=0,...  213 us
    all_gather x1, waiting for transfers between devices, body(): all_pairs = lax.all_gather(full_rows, 'integ', axis=1, tiled=True)[0]  78.9 us
    all_gather x1, waiting for transfers between devices, watch_tails(): local_now = lax.all_gather(state, axis_name=mesh_ax)  57.3 us
    dot_general x4, matrix products, body(): jnp.einsum('jqad,qbd->jab', weighted, factors, preferred_element_type=jnp...  21.8 us
    all_gather x1, blocking collectives, body(): full_rows = lax.all_gather(masked_block, 'virt', axis=2, tiled=True)  12.8 us
  transfers between devices with their start and end apart: 3, of which 3 were waited for; matrix products, arithmetic and copies ran while one was open for 8% of the time, Pallas kernels for 0%

profile of v1, /device:TPU:2, one launch (start us, length us, event | category | flops | bytes accessed | tf_op | source)
XLA Modules:
  0.0 410.9 jit_solution(14737095083376745069)
XLA Ops:
  6.5 0.0 copy-start
  6.5 0.0 all-gather.4.cloned.1.call-start
  6.5 0.7 convert_bitcast_fusion.2
  7.2 0.1 broadcast_bitcast_fusion
  7.3 0.1 dynamic_slice.32
  7.4 0.8 fusion.92
  8.2 12.8 %all_gather.12 = bf16[1,1,256,256]{3,2,1,0:T(8,128)(2,1)} all-gather(bf16[1,1,64,256]{3,2,1,0:T(8,128)(2,1)S(1)} %fusion.92), channel_id=1, replica_groups=mesh['pair'=2,'virt'=4,'integ'=32] {'virt'}, dimensions={2}, use_global_device_ids=true | all-gather | bytes 163840 | tf_op jit(solution)/shard_map/all_gather | solution.py:39
  21.0 0.0 all-gather.4.cloned.1.call-update
  21.1 0.0 all-gather.6.cloned.1.call-start
  21.1 0.9 constant_dynamic-slice_fusion
  22.1 0.1 copy.22
  22.2 0.0 copy-done
  22.2 1.6 fusion.89
  23.8 0.0 all-gather.6.cloned.1.call-update
  23.8 0.0 reduce-scatter.2.cloned.1.call-start
  23.8 0.7 convert_element_type.102
  24.5 0.3 broadcast_in_dim.10
  24.9 1.8 broadcast_multiply_fusion
  26.7 78.9 %all-gather.4.cloned.1.call-done = bf16[1,32,256,256]{3,2,0,1:T(8,128)(2,1)} async-done(((bf16[1,1,256,256]{3,2,0,1:T(8,128)(2,1)}), bf16[1,32,256,256]{3,2,0,1:T(8,128)(2,1)}) %all-gather.4.cloned.1.call-update) | async-done | bytes 4194320 | tf_op jit(solution)/shard_map/all_gather | solution.py:41
  105.6 5.4 %fusion.44 = bf16[8,64,256]{2,1,0:T(8,128)(2,1)S(1)} fusion(bf16[16,256,256]{2,1,0:T(8,128)(2,1)S(1)} %broadcast_multiply_fusion, bf16[1,32,256,256]{3,2,0,1:T(8,128)(2,1)} %all-gather.4.cloned.1.call-done, s32[]{:T(128)S(6)} %select_n.2), kind=kOutput, calls=%fused_computation.24 | convolution fusion | flops 2149711872 | bytes 3932164 | tf_op jit(solution)/shard_map/jqad,qbd->jab/dot_general | solution.py:54
  111.1 5.4 %fusion.49 = bf16[8,64,256]{2,1,0:T(8,128)(2,1)S(1)} fusion(bf16[16,256,256]{2,1,0:T(8,128)(2,1)S(1)} %broadcast_multiply_fusion, bf16[1,32,256,256]{3,2,0,1:T(8,128)(2,1)} %all-gather.4.cloned.1.call-done, s32[]{:T(128)S(6)} %select_n.2), kind=kOutput, calls=%fused_computation.25 | convolution fusion | flops 2149711872 | bytes 3932164 | tf_op jit(solution)/shard_map/jqad,qbd->jab/dot_general | solution.py:54
  116.5 5.5 %fusion.54 = bf16[8,64,256]{2,1,0:T(8,128)(2,1)S(1)} fusion(bf16[16,256,256]{2,1,0:T(8,128)(2,1)S(1)} %broadcast_multiply_fusion, bf16[1,32,256,256]{3,2,0,1:T(8,128)(2,1)} %all-gather.4.cloned.1.call-done, s32[]{:T(128)S(6)} %select_n.2), kind=kOutput, calls=%fused_computation.26 | convolution fusion | flops 2149711872 | bytes 3932164 | tf_op jit(solution)/shard_map/jqad,qbd->jab/dot_general | solution.py:54
  122.0 0.0 copy-start.1
  122.0 5.4 %fusion.59 = bf16[8,64,256]{2,1,0:T(8,128)(2,1)S(1)} fusion(bf16[16,256,256]{2,1,0:T(8,128)(2,1)S(1)} %broadcast_multiply_fusion, bf16[1,32,256,256]{3,2,0,1:T(8,128)(2,1)} %all-gather.4.cloned.1.call-done, s32[]{:T(128)S(6)} %select_n.2), kind=kOutput, calls=%fused_computation.27 | convolution fusion | flops 2149711872 | bytes 3932164 | tf_op jit(solution)/shard_map/jqad,qbd->jab/dot_general | solution.py:54
  127.5 1.1 pad_maximum_fusion
  128.6 0.0 reduce-scatter.2.cloned.1.call-update
  128.6 0.0 copy-done.1
  128.6 0.1 dynamic_slice.43
  130.0 57.3 %all-gather.6.cloned.1.call-done = f32[2048,512]{1,0:T(8,128)} async-done(((f32[64,512]{1,0:T(8,128)}), f32[2048,512]{1,0:T(8,128)}) %all-gather.6.cloned.1.call-update) | async-done | bytes 4194320 | tf_op jit(solution)/shard_map/all_gather | solution.py:62
  187.3 2.5 reduce_sum.9
  189.8 0.2 fusion.87
  190.0 212.8 %reduce-scatter.2.cloned.1.call-done = bf16[1,64,256]{2,1,0:T(8,128)(2,1)} async-done(((bf16[32,64,256]{2,1,0:T(8,128)(2,1)}), bf16[1,64,256]{2,1,0:T(8,128)(2,1)}) %reduce-scatter.2.cloned.1.call-update) | async-done | bytes 32784 | tf_op jit(solution)/shard_map/reduce_scatter | solution.py:57
  402.8 1.6 fusion.69
  (2 shorter events, 0.0 us)
Async XLA Ops:
  6.5 15.6 %copy-start = (bf16[512,1,256]{2,0,1:T(8,128)(2,1)S(1)}, bf16[512,1,256]{2,0,1:T(8,128)(2,1)}, u32[]{:S(2)}) copy-start(bf16[512,1,256]{2,0,1:T(8,128)(2,1)} %param.10) | copy-start | bytes 786436
  6.5 99.1 %all-gather.4.cloned.1.call-start = ((), (), s32[]{:S(2)}) async-start(), calls=%async_computation.1 | async-start | bytes 4325376 | tf_op jit(solution)/shard_map/all_gather | solution.py:41
  21.1 166.2 %all-gather.6.cloned.1.call-start = ((), (), s32[]{:S(2)}) async-start(), calls=%async_computation.3 | async-start | bytes 4325376 | tf_op jit(solution)/shard_map/all_gather | solution.py:62
  23.8 379.0 %reduce-scatter.2.cloned.1.call-start = ((), (), s32[]{:S(2)}) async-start(), calls=%async_computation.2 | async-start | bytes 1081344 | tf_op jit(solution)/shard_map/reduce_scatter | solution.py:57
  122.0 6.6 %copy-start.1 = (f32[256]{0:T(256)S(1)}, f32[256]{0:T(256)}, u32[]{:S(2)}) copy-start(f32[256]{0:T(256)} %param.13) | copy-start | bytes 3076
Sparse Core Ops, SparseCore 0:
  21.2 84.4 all-gather.3
  108.2 79.0 all-gather.5
  191.1 211.6 reduce-scatter.1
